TPU v7x, 32 devices: a whole 2x2x4 slice. The times are simulated.
32 devices in a mesh: region: 8 (over y, x, core), brick: 4 (over z).
Axes of the slice: x: 2, y: 2, z: 4, core: 2. Of those that a mesh axis runs over, the one named last changes fastest.
Arguments:
- velocity: float32 [3, 128, 64, 256], P(None, 'region', 'brick'), may hold values from -6 to 6
- viscosity: float32 [128, 64, 256], P('region', 'brick'), may hold values from 0.05 to 0.5
- marker_pos: float32 [3, 131072], P(None, ('region', 'brick')), as said below
- marker_force: float32 [3, 131072], P(None, ('region', 'brick')), may hold values from -240 to 240
- slot_lists: int32 [32, 8192], P(('region', 'brick')), may hold values from 0 to 16384, as said below
Outputs:
- predicted: float32 [3, 128, 64, 256], P(None, 'region', 'brick')
Inputs may be any that keep to these rules, and one draw needn't show every extreme that they name: `slot_lists`: each row lists, in increasing order, the indices within its region group's 16384 markers of the markers whose second coordinate lies in that brick's rows, then is padded with 16384; every marker of the group stands in exactly one row, and in every region group one row is full. `marker_pos`: the first coordinate of a marker lies 2 or more cells inside its region group's slab, the third 2 or more cells from the grid's ends, and the second within the rows of the brick whose slot row lists it.
All inputs are finite; a program needn't handle non-finite values.
Results may differ from a plain program's by a relative error of at most 0.00088.
Values sent between devices are 32-bit elements; how exact they have to be, the bound alone decides.
No kernel may reach another device: no remote copies, remote signals or barrier semaphores. Data moves between devices by JAX's collectives and lax.ppermute only.
A program may use at most 192 MiB of HBM per device.

v0:
```python
import jax
import jax.numpy as jnp
from jax import lax
from jax.sharding import PartitionSpec as P


def from_behind(x, axis, by):
    peers = lax.axis_size(axis)
    pairs = [(i, i + by) for i in range(peers) if 0 <= i + by < peers]
    return lax.ppermute(x, axis, pairs)


def extended_2(block, sides, width):
    for axis, dim in sides:
        count = lax.axis_size(axis)
        forward = [(i, i + 1) for i in range(count - 1)]
        backward = [(target, source) for source, target in forward]
        low = lax.ppermute(
            lax.slice_in_dim(block, block.shape[dim] - width, None, axis=dim), axis, forward
        )
        high = lax.ppermute(lax.slice_in_dim(block, 0, width, axis=dim), axis, backward)
        block = jnp.concatenate([low, block, high], axis=dim)
    return block


def kernel_weight(dist):
    return jnp.where(jnp.abs(dist) < 2.0, 0.25 * (1.0 + jnp.cos(0.5 * jnp.pi * dist)), 0.0)


def spread_rows(pos, force, row_low, rows, col_low, cols, depth):
    count = pos.shape[1]
    block = 1024
    x_centre = (col_low + jnp.arange(cols, dtype=jnp.int32)).astype(jnp.float32) + 0.5
    y_centre = (row_low + jnp.arange(rows, dtype=jnp.int32)).astype(jnp.float32) + 0.5
    z_centre = jnp.arange(depth, dtype=jnp.int32).astype(jnp.float32) + 0.5

    def one_block(turn, total):
        start = turn * block
        pos_part = lax.dynamic_slice_in_dim(pos, start, block, 1)
        force_part = lax.dynamic_slice_in_dim(force, start, block, 1)
        weight_x = kernel_weight(x_centre[:, None] - pos_part[0][None, :])
        weight_y = kernel_weight(y_centre[:, None] - pos_part[1][None, :])
        weight_z = kernel_weight(z_centre[None, :] - pos_part[2][:, None])
        factor = (
            force_part[:, None, None, :] * weight_x[None, :, None, :] * weight_y[None, None, :, :]
        )
        factor = factor.reshape(3 * cols * rows, block).astype(jnp.bfloat16)
        return total + jnp.dot(
            factor, weight_z.astype(jnp.bfloat16), preferred_element_type=jnp.float32
        )

    empty = jnp.zeros((3 * cols * rows, depth), jnp.float32)
    total = lax.fori_loop(0, count // block, one_block, empty)
    return total.reshape(3, cols, rows, depth)


def side(array, axis, offset):
    parts = [slice(1, -1), slice(1, -1), slice(1, -1)]
    size = array.shape[array.ndim - 3 + axis]
    parts[axis] = slice(1 + offset, size - 1 + offset)
    if array.ndim == 4:
        return array[:, parts[0], parts[1], parts[2]]
    return array[parts[0], parts[1], parts[2]]


def advance(padded, force_field):
    vel = padded[:3]
    visc = padded[3]
    speed = side(vel, 0, 0)
    visc_mid = side(visc, 0, 0)
    diffusion = jnp.zeros_like(speed)
    advection = jnp.zeros_like(speed)
    for axis in range(3):
        upper = side(vel, axis, 1)
        lower = side(vel, axis, -1)
        visc_up = side(visc, axis, 1)
        visc_dn = side(visc, axis, -1)
        diffusion = (
            diffusion
            + 0.5 * (visc_mid + visc_up) * (upper - speed)
            - 0.5 * (visc_mid + visc_dn) * (speed - lower)
        )
        advection = advection + speed[axis][None] * (upper - lower) * 0.5
    return speed + 0.1 * (diffusion - advection + force_field)


def body(velocity, viscosity, marker_pos, marker_force, slot_lists):
    cols, own_rows, depth = viscosity.shape
    region = lax.axis_index("region")
    brick = lax.axis_index("brick")
    own_slots = slot_lists[0]
    row_low = brick * own_rows - 2
    rows = own_rows + 4
    blank = jnp.zeros((3, own_slots.shape[0]), jnp.float32)
    start = jnp.int32(0)
    pos_piece = lax.all_gather(marker_pos, "brick", axis=1, tiled=True)
    force_piece = lax.all_gather(marker_force, "brick", axis=1, tiled=True)
    length = pos_piece.shape[1]
    inside = ((own_slots >= start) & (own_slots < start + length))[None, :]
    local = jnp.clip(own_slots, 0, length - 1)
    pos = jnp.where(inside, jnp.take(pos_piece, local, axis=1), blank)
    force = jnp.where(inside, jnp.take(force_piece, local, axis=1), blank)
    field = spread_rows(pos, force, row_low, rows, region * cols, cols, depth)
    upper_rim = field[:, :, own_rows + 2 :, :]
    lower_rim = field[:, :, :2, :]
    from_below = from_behind(upper_rim, "brick", 1)
    from_above = from_behind(lower_rim, "brick", -1)
    centre = field[:, :, 2 : own_rows + 2, :]
    centre = centre.at[:, :, :2, :].add(from_below)
    force_field = centre.at[:, :, own_rows - 2 :, :].add(from_above)
    stacked = jnp.concatenate([velocity, viscosity[None]], axis=0)
    extended = extended_2(stacked, (("region", 1), ("brick", 2)), 1)
    padded = jnp.pad(extended, ((0, 0), (0, 0), (0, 0), (1, 1)))
    return advance(padded, force_field)


def solution(mesh):
    placed = (
        P(None, "region", "brick", None),
        P("region", "brick", None),
        P(None, ("region", "brick")),
        P(None, ("region", "brick")),
        P(("region", "brick"), None),
    )
    return jax.shard_map(
        body,
        mesh=mesh,
        in_specs=placed,
        out_specs=P(None, "region", "brick", None),
        check_vma=False,
    )
```

profile of v0, /device:TPU:0, one launch (start us, length us, event | category | flops | bytes accessed | tf_op | source)
XLA Modules:
  0.0 467.4 jit_solution(8026704652510305181)
XLA Ops:
  0.0 0.8 broadcast_clamp_fusion
  0.8 0.9 and_reduce_fusion
  1.7 1.5 copy.10
  3.2 141.2 %all_gather.6 = f32[3,16384]{0,1:T(8,128)} all-gather(f32[3,4096]{0,1:T(8,128)S(1)} %copy.10), channel_id=1, replica_groups=mesh['region'=8,'brick'=4] {'brick'}, dimensions={1}, use_global_device_ids=true | all-gather | bytes 245760 | tf_op jit(solution)/shard_map/all_gather | solution.py:97
  144.4 0.6 copy.11
  145.1 139.4 %all_gather.7 = f32[3,16384]{0,1:T(8,128)} all-gather(f32[3,4096]{0,1:T(8,128)S(1)} %copy.11), channel_id=1, replica_groups=mesh['region'=8,'brick'=4] {'brick'}, dimensions={1}, use_global_device_ids=true | all-gather | bytes 245760 | tf_op jit(solution)/shard_map/all_gather | solution.py:96
  284.5 31.2 %gather_fusion = f32[8192,3]{1,0:T(8,128)} fusion(f32[3,16384]{0,1:T(8,128)} %all_gather.6, s32[8192]{0:T(1024)S(1)} %fusion.44), kind=kCustom, calls=%fused_computation.clone | custom fusion | bytes 229376 | tf_op jit(solution)/shard_map/jit(_take)/gather | solution.py:102
  315.7 31.3 %gather_fusion.1 = f32[8192,3]{1,0:T(8,128)} fusion(f32[3,16384]{0,1:T(8,128)} %all_gather.7, s32[8192]{0:T(1024)S(1)} %fusion.44), kind=kCustom, calls=%fused_computation.1.clone | custom fusion | bytes 229376 | tf_op jit(solution)/shard_map/jit(_take)/gather | solution.py:101
  347.0 8.0 %bitcast_select_fusion = (f32[3,8192]{0,1:T(8,128)}, f32[3,8192]{0,1:T(8,128)}) fusion(f32[8192,3]{1,0:T(8,128)} %gather_fusion.1, pred[8192]{0:T(1024)(128)(4,1)S(1)} %compare_and_fusion, pred[8192]{0:T(1024)(128)(4,1)S(1)} %and_reduce_fusion, f32[8192,3]{1,0:T(8,128)} %gather_fusion), kind=kLoop, calls=%fused_computation.47 | loop fusion | flops 98304 | bytes 409600 | tf_op jit(solution)/shard_map/jit(_where)/select_n | solution.py:101
  355.0 2.8 copy.12
  357.8 2.9 copy.13
  360.7 79.9 %while.16 = (s32[]{:T(128)}, f32[960,256]{1,0:T(8,128)S(1)}, f32[3,8192]{1,0:T(4,128)S(1)}, f32[3,8192]{1,0:T(4,128)S(1)}, s32[]{:T(128)}, /*index=5*/s32[]{:T(1...) while((s32[]{:T(128)}, f32[960,256]{1,0:T(8,128)S(1)}, ...), condition=%wide.region_1.3_spmd.clone, body=%wide.region_0.2_spmd.clone.sunk | while | flops 508179072 | bytes 11381301 | solution.py:53
  361.8 0.6 multiply_convert_fusion.2
  362.4 2.0 convert_element_type.63
  364.4 6.3 %convolution_add_fusion.2 = f32[960,256]{1,0:T(8,128)S(1)} fusion(bf16[960,1024]{1,0:T(8,128)(2,1)} %convert_element_type.63, f32[960,256]{1,0:T(8,128)S(1)} %get-tuple-element.284, f32[1024]{0:T(1024)S(1)} %bitcast.34, f32[256]{0:T(256)S(1)} %convert_add_fusion.8, pred[]{:T(512)S(6)} %compare.35), kind=kOutput, calls=%fused_computation.8.clone.1 | convolution fusion | flops 505905152 | bytes 3937281 | tf_op jit(solution)/shard_map/while/body/eval_jaxpr/dot_general | solution.py:48
  371.8 0.6 multiply_convert_fusion.2
  372.4 2.0 convert_element_type.63
  374.4 6.2 %convolution_add_fusion.2 = f32[960,256]{1,0:T(8,128)S(1)} fusion(bf16[960,1024]{1,0:T(8,128)(2,1)} %convert_element_type.63, f32[960,256]{1,0:T(8,128)S(1)} %get-tuple-element.284, f32[1024]{0:T(1024)S(1)} %bitcast.34, f32[256]{0:T(256)S(1)} %convert_add_fusion.8, pred[]{:T(512)S(6)} %compare.35), kind=kOutput, calls=%fused_computation.8.clone.1 | convolution fusion | flops 505905152 | bytes 3937281 | tf_op jit(solution)/shard_map/while/body/eval_jaxpr/dot_general | solution.py:48
  381.4 0.4 fusion.56
  381.8 0.6 multiply_convert_fusion.2
  382.4 2.0 convert_element_type.63
  384.4 6.3 %convolution_add_fusion.2 = f32[960,256]{1,0:T(8,128)S(1)} fusion(bf16[960,1024]{1,0:T(8,128)(2,1)} %convert_element_type.63, f32[960,256]{1,0:T(8,128)S(1)} %get-tuple-element.284, f32[1024]{0:T(1024)S(1)} %bitcast.34, f32[256]{0:T(256)S(1)} %convert_add_fusion.8, pred[]{:T(512)S(6)} %compare.35), kind=kOutput, calls=%fused_computation.8.clone.1 | convolution fusion | flops 505905152 | bytes 3937281 | tf_op jit(solution)/shard_map/while/body/eval_jaxpr/dot_general | solution.py:48
  391.8 0.6 multiply_convert_fusion.2
  392.4 2.0 convert_element_type.63
  394.4 6.3 %convolution_add_fusion.2 = f32[960,256]{1,0:T(8,128)S(1)} fusion(bf16[960,1024]{1,0:T(8,128)(2,1)} %convert_element_type.63, f32[960,256]{1,0:T(8,128)S(1)} %get-tuple-element.284, f32[1024]{0:T(1024)S(1)} %bitcast.34, f32[256]{0:T(256)S(1)} %convert_add_fusion.8, pred[]{:T(512)S(6)} %compare.35), kind=kOutput, calls=%fused_computation.8.clone.1 | convolution fusion | flops 505905152 | bytes 3937281 | tf_op jit(solution)/shard_map/while/body/eval_jaxpr/dot_general | solution.py:48
  401.8 0.6 multiply_convert_fusion.2
  402.4 2.0 convert_element_type.63
  404.4 6.2 %convolution_add_fusion.2 = f32[960,256]{1,0:T(8,128)S(1)} fusion(bf16[960,1024]{1,0:T(8,128)(2,1)} %convert_element_type.63, f32[960,256]{1,0:T(8,128)S(1)} %get-tuple-element.284, f32[1024]{0:T(1024)S(1)} %bitcast.34, f32[256]{0:T(256)S(1)} %convert_add_fusion.8, pred[]{:T(512)S(6)} %compare.35), kind=kOutput, calls=%fused_computation.8.clone.1 | convolution fusion | flops 505905152 | bytes 3937281 | tf_op jit(solution)/shard_map/while/body/eval_jaxpr/dot_general | solution.py:48
  411.7 0.6 multiply_convert_fusion.2
  412.4 2.0 convert_element_type.63
  414.4 6.3 %convolution_add_fusion.2 = f32[960,256]{1,0:T(8,128)S(1)} fusion(bf16[960,1024]{1,0:T(8,128)(2,1)} %convert_element_type.63, f32[960,256]{1,0:T(8,128)S(1)} %get-tuple-element.284, f32[1024]{0:T(1024)S(1)} %bitcast.34, f32[256]{0:T(256)S(1)} %convert_add_fusion.8, pred[]{:T(512)S(6)} %compare.35), kind=kOutput, calls=%fused_computation.8.clone.1 | convolution fusion | flops 505905152 | bytes 3937281 | tf_op jit(solution)/shard_map/while/body/eval_jaxpr/dot_general | solution.py:48
  421.7 0.6 multiply_convert_fusion.2
  422.4 2.0 convert_element_type.63
  424.4 6.2 %convolution_add_fusion.2 = f32[960,256]{1,0:T(8,128)S(1)} fusion(bf16[960,1024]{1,0:T(8,128)(2,1)} %convert_element_type.63, f32[960,256]{1,0:T(8,128)S(1)} %get-tuple-element.284, f32[1024]{0:T(1024)S(1)} %bitcast.34, f32[256]{0:T(256)S(1)} %convert_add_fusion.8, pred[]{:T(512)S(6)} %compare.35), kind=kOutput, calls=%fused_computation.8.clone.1 | convolution fusion | flops 505905152 | bytes 3937281 | tf_op jit(solution)/shard_map/while/body/eval_jaxpr/dot_general | solution.py:48
  431.7 0.6 multiply_convert_fusion.2
  432.4 2.0 convert_element_type.63
  434.4 6.3 %convolution_add_fusion.2 = f32[960,256]{1,0:T(8,128)S(1)} fusion(bf16[960,1024]{1,0:T(8,128)(2,1)} %convert_element_type.63, f32[960,256]{1,0:T(8,128)S(1)} %get-tuple-element.284, f32[1024]{0:T(1024)S(1)} %bitcast.34, f32[256]{0:T(256)S(1)} %convert_add_fusion.8, pred[]{:T(512)S(6)} %compare.35), kind=kOutput, calls=%fused_computation.8.clone.1 | convolution fusion | flops 505905152 | bytes 3937281 | tf_op jit(solution)/shard_map/while/body/eval_jaxpr/dot_general | solution.py:48
  440.9 2.9 collective-permute-start.4
  443.7 1.3 collective-permute-start.5
  445.1 1.6 collective-permute-start
  446.7 1.3 collective-permute-start.1
  448.2 3.1 collective-permute-done.1
  451.3 4.5 collective-permute-start.2
  455.9 1.5 collective-permute-start.3
  457.9 4.8 %collective-permute-done.3 = f32[4,18,1,256]{3,2,1,0:T(1,128)S(1)} collective-permute-done((f32[4,18,1,256]{3,2,1,0:T(1,128)S(1)}, f32[4,18,1,256]{3,2,1,0:T(1,128)S(1)}, u32[]{:S(2)}, u32[]{:S(2)}) %collective-permute-start.3) | collective-permute-done | bytes 73760 | tf_op jit(solution)/shard_map/ppermute | solution.py:21
  462.7 1.3 select_maximum_fusion
  464.1 0.5 fusion.41
  464.6 2.8 multiply_add_fusion
  (117 shorter events, 8.8 us)
Async XLA Ops:
  3.2 141.2 %copy-start.4 = (f32[3,4096]{1,0:T(4,128)S(1)}, f32[3,4096]{1,0:T(4,128)}, u32[]{:S(2)}) copy-start(f32[3,4096]{1,0:T(4,128)} %param.15) | copy-start | bytes 147460
  360.7 0.7 copy-start.2
  364.4 6.3 %copy-start.3 = (f32[3,8192]{1,0:T(4,128)S(1)}, f32[3,8192]{1,0:T(4,128)}, u32[]{:S(2)}) copy-start(f32[3,8192]{1,0:T(4,128)} %copy-done.2) | copy-start | bytes 294916 | tf_op jit(solution)/shard_map/while
  370.7 0.7 copy-start.2
  374.4 6.3 %copy-start.3 = (f32[3,8192]{1,0:T(4,128)S(1)}, f32[3,8192]{1,0:T(4,128)}, u32[]{:S(2)}) copy-start(f32[3,8192]{1,0:T(4,128)} %copy-done.2) | copy-start | bytes 294916 | tf_op jit(solution)/shard_map/while
  380.7 0.7 copy-start.2
  384.4 6.3 %copy-start.3 = (f32[3,8192]{1,0:T(4,128)S(1)}, f32[3,8192]{1,0:T(4,128)}, u32[]{:S(2)}) copy-start(f32[3,8192]{1,0:T(4,128)} %copy-done.2) | copy-start | bytes 294916 | tf_op jit(solution)/shard_map/while
  390.7 0.7 copy-start.2
  394.4 6.3 %copy-start.3 = (f32[3,8192]{1,0:T(4,128)S(1)}, f32[3,8192]{1,0:T(4,128)}, u32[]{:S(2)}) copy-start(f32[3,8192]{1,0:T(4,128)} %copy-done.2) | copy-start | bytes 294916 | tf_op jit(solution)/shard_map/while
  400.7 0.7 copy-start.2
  404.4 6.3 %copy-start.3 = (f32[3,8192]{1,0:T(4,128)S(1)}, f32[3,8192]{1,0:T(4,128)}, u32[]{:S(2)}) copy-start(f32[3,8192]{1,0:T(4,128)} %copy-done.2) | copy-start | bytes 294916 | tf_op jit(solution)/shard_map/while
  410.7 0.7 copy-start.2
  414.4 6.3 %copy-start.3 = (f32[3,8192]{1,0:T(4,128)S(1)}, f32[3,8192]{1,0:T(4,128)}, u32[]{:S(2)}) copy-start(f32[3,8192]{1,0:T(4,128)} %copy-done.2) | copy-start | bytes 294916 | tf_op jit(solution)/shard_map/while
  420.7 0.7 copy-start.2
  424.4 6.3 %copy-start.3 = (f32[3,8192]{1,0:T(4,128)S(1)}, f32[3,8192]{1,0:T(4,128)}, u32[]{:S(2)}) copy-start(f32[3,8192]{1,0:T(4,128)} %copy-done.2) | copy-start | bytes 294916 | tf_op jit(solution)/shard_map/while
  430.7 0.7 copy-start.2
  434.4 6.3 %copy-start.3 = (f32[3,8192]{1,0:T(4,128)S(1)}, f32[3,8192]{1,0:T(4,128)}, u32[]{:S(2)}) copy-start(f32[3,8192]{1,0:T(4,128)} %copy-done.2) | copy-start | bytes 294916 | tf_op jit(solution)/shard_map/while
  440.6 4.4 copy-start
  440.7 4.4 copy-start.1
  440.9 16.5 %collective-permute-start.4 = (f32[3,16,2,256]{3,2,1,0:T(2,128)S(1)}, f32[3,16,2,256]{3,2,1,0:T(2,128)S(1)}, u32[]{:S(2)}, u32[]{:S(2)}) collective-permute-start(f32[3,16,2,256]{3,2,1,0:T(2,128)S(1)} %get-tuple-element.214), channel_id=1, source_target_pairs={{0,1},{1,2},{2,3},{4,5},{5,6},{6,7},{8,9},{9,10},{10,11},{12,13},{... | collective-permute-start | bytes 294920 | tf_op jit(solution)/shard_map/ppermute | solution.py:10
  443.7 13.8 %collective-permute-start.5 = (f32[3,16,2,256]{3,2,1,0:T(2,128)S(1)}, f32[3,16,2,256]{3,2,1,0:T(2,128)S(1)}, u32[]{:S(2)}, u32[]{:S(2)}) collective-permute-start(f32[3,16,2,256]{3,2,1,0:T(2,128)S(1)} %get-tuple-element.213), channel_id=1, source_target_pairs={{1,0},{2,1},{3,2},{5,4},{6,5},{7,6},{9,8},{10,9},{11,10},{13,12},{... | collective-permute-start | bytes 294920 | tf_op jit(solution)/shard_map/ppermute | solution.py:10
  445.1 3.1 collective-permute-start
  446.7 4.5 collective-permute-start.1
  451.3 6.5 %collective-permute-start.2 = (f32[4,18,1,256]{3,2,1,0:T(1,128)S(1)}, f32[4,18,1,256]{3,2,1,0:T(1,128)S(1)}, u32[]{:S(2)}, u32[]{:S(2)}) collective-permute-start(f32[4,18,1,256]{3,2,1,0:T(1,128)S(1)} %get-tuple-element.211), channel_id=1, source_target_pairs={{0,1},{1,2},{2,3},{4,5},{5,6},{6,7},{8,9},{9,10},{10,11},{12,13},{... | collective-permute-start | bytes 221192 | tf_op jit(solution)/shard_map/ppermute | solution.py:18
  455.9 6.8 %collective-permute-start.3 = (f32[4,18,1,256]{3,2,1,0:T(1,128)S(1)}, f32[4,18,1,256]{3,2,1,0:T(1,128)S(1)}, u32[]{:S(2)}, u32[]{:S(2)}) collective-permute-start(f32[4,18,1,256]{3,2,1,0:T(1,128)S(1)} %get-tuple-element.212), channel_id=1, source_target_pairs={{1,0},{2,1},{3,2},{5,4},{6,5},{7,6},{9,8},{10,9},{11,10},{13,12},{... | collective-permute-start | bytes 221192 | tf_op jit(solution)/shard_map/ppermute | solution.py:21
where the time goes:
time: 470 us; the launch traced here: 467 us
  blocking collectives  281 us (60%)
  local copies, waits for them, and re-layouts  88.8 us (19%)
  matrix products  50 us (11%)
  other arithmetic  25.7 us (5%)
  starting transfers between devices  13.1 us (3%)
  waiting for transfers between devices  8.14 us (2%)
    all_gather x1, blocking collectives, body(): force_piece = lax.all_gather(marker_force, 'brick', axis=1, tiled=True)  141 us
    all_gather x1, blocking collectives, body(): pos_piece = lax.all_gather(marker_pos, 'brick', axis=1, tiled=True)  139 us
    dot_general x8, matrix products, one_block(): jnp.dot(factor, weight_z.astype(jnp.bfloat16), preferred_element_type=jnp...  50 us
    gather x1, local copies, waits for them, and re-layouts, body(): pos = jnp.where(inside, jnp.take(pos_piece, local, axis=1), blank)  31.3 us
    gather x1, local copies, waits for them, and re-layouts, body(): force = jnp.where(inside, jnp.take(force_piece, local, axis=1), blank)  31.2 us
    convert_element_type x8, local copies, waits for them, and re-layouts, one_block(): factor = factor.reshape(3 * cols * rows, block).astype(jnp.bfloat16)  16 us
  transfers between devices with their start and end apart: 6, of which 3 were waited for; matrix products, arithmetic and copies ran while one was open for 0% of the time, Pallas kernels for 0%

commit v1 on v0

v1 whole, which is shorter than its diff:
```python
import functools
import math

import jax
import jax.numpy as jnp
from jax import lax
from jax.experimental import pallas as pl
from jax.experimental.pallas import tpu as pltpu
from jax.sharding import PartitionSpec as P

LANES = 128
TILE = 2 * LANES
NQ = 24


def poly(t, coefs):
    out = jnp.full_like(t, coefs[-1])
    for c in coefs[-2::-1]:
        out = out * t + c
    return out


COS_COEFS = [(-1.0) ** n / math.factorial(2 * n) for n in range(8)]
SIN_COEFS = [(-1.0) ** n / math.factorial(2 * n + 1) for n in range(8)]


def window(u):
    shifted = u - 0.5
    cell = jnp.floor(shifted)
    angle = (0.5 * math.pi) * (shifted - cell)
    sq = angle * angle
    cosine = poly(sq, COS_COEFS)
    sine = angle * poly(sq, SIN_COEFS)
    first = cell - 1.0
    weights = (0.25 - 0.25 * sine, 0.25 + 0.25 * cosine, 0.25 + 0.25 * sine, 0.25 - 0.25 * cosine)
    residue = first - 4.0 * jnp.floor(first * 0.25)
    is_res = [residue == float(m) for m in range(4)]
    by_res = []
    for m in range(4):
        w = weights[3]
        for a in (2, 1, 0):
            w = jnp.where(is_res[(m - a) % 4], weights[a], w)
        by_res.append(w)
    return first, by_res


def prepare(mk_ref, prep_ref, groups, x_low, y_low):
    def part(q):
        return mk_ref[q * groups:(q + 1) * groups, :]

    def put(q, value):
        prep_ref[q * groups:(q + 1) * groups, :] = value

    z_first, z_w = window(part(2))
    block = jnp.floor(z_first * (1.0 / 16.0))
    put(0, block)
    put(1, z_first - 16.0 * block)
    for m in range(4):
        put(2 + m, z_w[m])
    y_first, y_w = window(part(1) - y_low)
    put(6, y_first)
    for m in range(4):
        put(7 + m, y_w[m])
    x_first, x_w = window(part(0) - x_low)
    put(11, x_first)
    for c in range(3):
        force = part(3 + c)
        for m in range(4):
            put(12 + 4 * c + m, force * x_w[m])


def add_tile(prep_ref, groups, tile, mxu, accs, cols, rows, depth):
    sub = lax.broadcasted_iota(jnp.int32, (8, LANES), 0)
    subf = sub.astype(jnp.float32)
    phase = sub & 3
    zero16 = jnp.zeros((16, LANES), jnp.bfloat16)

    def wide(q, g):
        return jnp.broadcast_to(prep_ref[pl.ds(q * groups + g, 1), :], (8, LANES))

    def pattern(q, g):
        w = wide(q + 3, g)
        for m in (2, 1, 0):
            w = jnp.where(phase == m, wide(q + m, g), w)
        return w

    def packed(a, b):
        return jnp.concatenate([a, b], axis=0).astype(jnp.bfloat16)

    halves = [2 * tile, 2 * tile + 1]
    zcols = []
    for g in halves:
        w = pattern(2, g)
        off = wide(1, g)
        zero = jnp.zeros_like(w)
        d0 = subf - off
        lo0 = jnp.where((d0 >= 0.0) & (d0 <= 3.0), w, zero)
        lo1 = jnp.where((d0 >= -8.0) & (d0 <= -5.0), w, zero)
        hi0 = jnp.where(d0 <= -13.0, w, zero)
        low = packed(lo0, lo1)
        high = packed(hi0, zero)
        blk = wide(0, g)
        blk16 = packed(blk, blk)
        prev = None
        col = []
        for t in range(depth // 16):
            here = blk16 == jnp.bfloat16(t)
            v = zero16 if prev is None else jnp.where(prev, high, zero16)
            col.append(jnp.where(here, low, v))
            prev = here
        zcols.append(jnp.concatenate(col, axis=0))
    pltpu.matmul_push_rhs(jnp.concatenate(zcols, axis=1), 0, mxu, transpose=True)

    wys = []
    xfirst = []
    for g in halves:
        w = pattern(7, g)
        zero = jnp.zeros_like(w)
        d0 = subf - wide(6, g)
        pair = []
        for h in range(rows // 8):
            d = d0 + 8.0 * h
            pair.append(jnp.where((d >= 0.0) & (d <= 3.0), w, zero))
        wys.append(pair)
        xf = wide(11, g)
        xfirst.append(packed(xf, xf))

    first = True
    for m in range(4):
        masks = {}
        for i in range(m, cols, 4):
            masks[i] = [
                (xf <= jnp.bfloat16(i)) & (xf >= jnp.bfloat16(i - 3)) for xf in xfirst
            ]
        for c in range(3):
            fx = [wide(12 + 4 * c + m, g) for g in halves]
            for rb in range(rows // 16):
                quad = [
                    packed(fx[n] * wys[n][2 * rb], fx[n] * wys[n][2 * rb + 1]) for n in range(2)
                ]
                for i in range(m, cols, 4):
                    lhs = jnp.concatenate(
                        [jnp.where(masks[i][n], quad[n], zero16) for n in range(2)], axis=1
                    )
                    pltpu.matmul_acc_lhs(
                        accs[(c * cols + i) * (rows // 16) + rb], lhs,
                        load_staged_rhs=0 if first else None,
                    )
                    first = False


def add_shard(mk_ref, prep_ref, accs, groups, x_low, y_low, cols, rows, depth):
    prepare(mk_ref, prep_ref, groups, x_low, y_low)

    def pair(t, carry):
        for mxu in range(2):
            add_tile(prep_ref, groups, 2 * t + mxu, mxu, accs[mxu], cols, rows, depth)
        return carry

    lax.fori_loop(0, groups // 4, pair, 0)


def corner(axes, cols, rows):
    region = lax.axis_index("region")
    brick = lax.axis_index("brick")
    return (region * cols).astype(jnp.float32), (brick * rows).astype(jnp.float32)


def pack_kernel(bricks, vel_ref, visc_ref, pos_ref, force_ref, mk_ref, s1_ref, s3_ref, xa_ref, xb_ref):
    cols, rows, depth = visc_ref.shape
    groups = pos_ref.shape[1] // LANES
    brick_odd = (lax.axis_index("brick") & 1) == 1
    region_odd = (lax.axis_index("region") & 1) == 1
    for c in range(3):
        for g in range(groups):
            lane = slice(g * LANES, (g + 1) * LANES)
            for src, q in ((pos_ref, c), (force_ref, 3 + c)):
                row = src[c:c + 1, lane]
                at = q * groups + g
                mk_ref[at:at + 1, :] = row
                s1_ref[at:at + 1, :] = row
                s3_ref[at:at + 1, :] = row

    def plane(c, i):
        return vel_ref[c, i] if c < 3 else visc_ref[i]

    base = 6 * groups
    for c in range(4):
        low, high = plane(c, 0), plane(c, cols - 1)
        xa_ref[c] = jnp.where(region_odd, low, high)
        xb_ref[c] = jnp.where(region_odd, high, low)
        for i in range(cols):
            p = plane(c, i)
            low, high = p[:1], p[rows - 1:rows]
            one = jnp.where(brick_odd, low, high)
            other = jnp.where(brick_odd, high, low)
            for h in range(depth // LANES):
                at = base + (h * 4 + c) * cols + i
                lane = slice(h * LANES, (h + 1) * LANES)
                s1_ref[at:at + 1, :] = one[:, lane]
                s3_ref[at:at + 1, :] = other[:, lane]


def pop(accs, index):
    return pltpu.matmul_pop(accs[0][index]) + pltpu.matmul_pop(accs[1][index])


def with_accumulators(kernel, naccs, depth, *refs):
    def run(*accs):
        kernel((accs[:naccs], accs[naccs:]), *refs)

    pl.run_scoped(
        run,
        *(pltpu.ACC(mxu)((16, depth), jnp.float32) for mxu in range(2) for _ in range(naccs)),
    )


def own_kernel(accs, vel_ref, visc_ref, mk_ref, base_ref, prep_ref):
    cols, rows, depth = visc_ref.shape
    groups = mk_ref.shape[0] // 6
    x_low, y_low = corner(None, cols, rows)
    add_shard(mk_ref, prep_ref, accs, groups, x_low, y_low, cols, rows, depth)
    lane = lax.broadcasted_iota(jnp.int32, (rows, depth), 1)
    row = lax.broadcasted_iota(jnp.int32, (rows, depth), 0)
    zero = jnp.zeros((rows, depth), jnp.float32)

    def around(p):
        jp = jnp.where(row == rows - 1, zero, pltpu.roll(p, rows - 1, 0))
        jm = jnp.where(row == 0, zero, pltpu.roll(p, 1, 0))
        kp = jnp.where(lane == depth - 1, zero, pltpu.roll(p, depth - 1, 1))
        km = jnp.where(lane == 0, zero, pltpu.roll(p, 1, 1))
        return jp, jm, kp, km

    for i in range(cols):
        mu = visc_ref[i]
        mu_ip = visc_ref[i + 1] if i + 1 < cols else zero
        mu_im = visc_ref[i - 1] if i > 0 else zero
        mu_all = (mu_ip, mu_im) + around(mu)
        v = [vel_ref[d, i] for d in range(3)]
        plus = [0.5 * ((mu + mu_all[2 * d]) - v[d]) for d in range(3)]
        minus = [0.5 * ((mu + mu_all[2 * d + 1]) + v[d]) for d in range(3)]
        total = 3.0 * mu
        for d in range(6):
            total = total + 0.5 * mu_all[d]
        for c in range(3):
            u = v[c]
            ip = vel_ref[c, i + 1] if i + 1 < cols else zero
            im = vel_ref[c, i - 1] if i > 0 else zero
            near = (ip, im) + around(u)
            sum_ = -(total * u)
            for d in range(3):
                sum_ = sum_ + plus[d] * near[2 * d] + minus[d] * near[2 * d + 1]
            base_ref[c, i] = u + 0.1 * (sum_ + pop(accs, c * cols + i))


def final_kernel(nfaces, accs, base_ref, s1_ref, s3_ref, xa_ref, xb_ref, ra_ref, rb_ref, *refs):
    *shards, out_ref, prep_ref = refs
    _, cols, rows, depth = base_ref.shape
    groups = (s1_ref.shape[0] - 8 * cols) // 6
    x_low, y_low = corner(None, cols, rows)
    for mk_ref in shards:
        add_shard(mk_ref, prep_ref, accs, groups, x_low, y_low, cols, rows, depth)

    region = lax.axis_index("region")
    regions = lax.axis_size("region")
    brick = lax.axis_index("brick")
    region_odd = (region & 1) == 1
    brick_odd = (brick & 1) == 1
    has_low = region > 0
    has_high = region < regions - 1

    for c in range(3):
        for i in range(cols):
            out_ref[c, i] = base_ref[c, i] + 0.1 * pop(accs, c * cols + i)

    def fix(sign, mu, mu_n, speed, u, u_n):
        along = speed if sign < 0 else -speed
        return 0.05 * ((mu + mu_n + along) * u_n - mu_n * u)

    zero = jnp.zeros((rows, depth), jnp.float32)
    own_high = [jnp.where(region_odd, xb_ref[c], xa_ref[c]) for c in range(4)]
    own_low = [jnp.where(region_odd, xa_ref[c], xb_ref[c]) for c in range(4)]
    far_high = [jnp.where(has_high, jnp.where(region_odd, rb_ref[c], ra_ref[c]), zero) for c in range(4)]
    far_low = [jnp.where(has_low, jnp.where(region_odd, ra_ref[c], rb_ref[c]), zero) for c in range(4)]
    for c in range(3):
        out_ref[c, cols - 1] += fix(1, own_high[3], far_high[3], own_high[0], own_high[c], far_high[c])
        out_ref[c, 0] += fix(-1, own_low[3], far_low[3], own_low[0], own_low[c], far_low[c])

    base = 6 * groups

    def face(ref, h, c):
        return ref[base + (h * 4 + c) * cols:base + (h * 4 + c + 1) * cols, :]

    none = jnp.zeros((cols, LANES), jnp.float32)
    for h in range(depth // LANES):
        lane = slice(h * LANES, (h + 1) * LANES)
        own_one = [face(s1_ref, h, c) for c in range(4)]
        own_two = [face(s3_ref, h, c) for c in range(4)]
        far_one = [face(shards[0], h, c) for c in range(4)] if nfaces else [none] * 4
        far_two = [none] * 4
        for t in range(1, nfaces):
            index = 2 ** (t + 1) - 2
            partner = brick ^ (index + 1)
            good = (partner - brick == 1) | (brick - partner == 1)
            far_two = [
                jnp.where(good, face(shards[index], h, c), far_two[c]) for c in range(4)
            ]
        high_own = [jnp.where(brick_odd, b, a) for a, b in zip(own_one, own_two)]
        low_own = [jnp.where(brick_odd, a, b) for a, b in zip(own_one, own_two)]
        high_far = [jnp.where(brick_odd, b, a) for a, b in zip(far_one, far_two)]
        low_far = [jnp.where(brick_odd, a, b) for a, b in zip(far_one, far_two)]
        for c in range(3):
            top = fix(1, high_own[3], high_far[3], high_own[1], high_own[c], high_far[c])
            low = fix(-1, low_own[3], low_far[3], low_own[1], low_own[c], low_far[c])
            for i in range(cols):
                out_ref[c, i, rows - 1:rows, lane] += top[i:i + 1]
                out_ref[c, i, 0:1, lane] += low[i:i + 1]


def body(velocity, viscosity, marker_pos, marker_force, slot_lists):
    del slot_lists
    cols, rows, depth = viscosity.shape
    bricks = lax.axis_size("brick")
    regions = lax.axis_size("region")
    groups = marker_pos.shape[1] // LANES
    f32 = jnp.float32
    vmem = pl.BlockSpec(memory_space=pltpu.VMEM)
    markers = jax.ShapeDtypeStruct((6 * groups, LANES), f32)
    with_face = jax.ShapeDtypeStruct((6 * groups + 8 * cols, LANES), f32)
    xface = jax.ShapeDtypeStruct((4, rows, depth), f32)
    mk, s1, s3, xa, xb = pl.pallas_call(
        functools.partial(pack_kernel, bricks),
        out_shape=(markers, with_face, with_face, xface, xface),
        in_specs=[vmem] * 4,
        out_specs=(vmem,) * 5,
        name="pack",
    )(velocity, viscosity, marker_pos, marker_force)

    partners = list(range(1, bricks))
    nfaces = 0
    received = {}
    for m in sorted(partners, key=lambda m: (m & (m + 1)) == 0):
        pairs = [(b, b ^ m) for b in range(bricks)]
        value = mk
        if m & (m + 1) == 0:
            value = s1 if m == 1 else s3
            nfaces += 1
        received[m] = lax.ppermute(value, "brick", pairs)
    ra = lax.ppermute(xa, "region", [(r, r ^ 1) for r in range(regions)])
    rb = lax.ppermute(
        xb, "region", [(r, (r + (1 if r % 2 else -1)) % regions) for r in range(regions)]
    )

    naccs = 3 * cols * rows // 16
    scratch = [pltpu.VMEM((NQ * groups, LANES), f32)]
    field = jax.ShapeDtypeStruct(velocity.shape, f32)
    base = pl.pallas_call(
        functools.partial(with_accumulators, own_kernel, naccs, depth),
        out_shape=field,
        in_specs=[vmem] * 3,
        out_specs=vmem,
        scratch_shapes=scratch,
        name="own",
    )(velocity, viscosity, mk)

    shards = [received[m] for m in partners]
    return pl.pallas_call(
        functools.partial(
            with_accumulators, functools.partial(final_kernel, nfaces), naccs, depth
        ),
        out_shape=field,
        in_specs=[vmem] * (7 + len(shards)),
        out_specs=vmem,
        scratch_shapes=scratch,
        name="final",
    )(base, s1, s3, xa, xb, ra, rb, *shards)


def solution(mesh):
    placed = (
        P(None, "region", "brick", None),
        P("region", "brick", None),
        P(None, ("region", "brick")),
        P(None, ("region", "brick")),
        P(("region", "brick"), None),
    )
    return jax.shard_map(
        body,
        mesh=mesh,
        in_specs=placed,
        out_specs=P(None, "region", "brick", None),
        check_vma=False,
    )
```

time: 470 us -> 31.5 us (0.07)
  blocking collectives: 281 us -> 0 us
  local copies, waits for them, and re-layouts: 88.8 us -> 1.34 us
  matrix products: 50 us -> 0 us
  other arithmetic: 25.7 us -> 0 us
  Pallas kernels: 0 us -> 18.1 us
  starting transfers between devices: 13.1 us -> 8.21 us
    all_gather x2 -> x0, blocking collectives: 281 us -> none  [the longest x1 141 us: body(): force_piece = lax.all_gather(marker_force, 'brick', axis=1, tiled=True)]
    gather x2 -> x0, local copies, waits for them, and re-layouts: 62.5 us -> none  [the longest x1 31.3 us: body(): pos = jnp.where(inside, jnp.take(pos_piece, local, axis=1), blank)]
    dot_general x8 -> x0, matrix products: 50 us -> none  [one_block(): jnp.dot(factor, weight_z.astype(jnp.bfloat16), preferred_element_type=jnp...]
    pallas_call x0 -> x3, Pallas kernels: none -> 18.1 us  [the longest x1 10.2 us: body(): pl.pallas_call(functools.partial(with_accumulators, functools.partial(fin...]
    convert_element_type x8 -> x0, local copies, waits for them, and re-layouts: 16 us -> none  [one_block(): factor = factor.reshape(3 * cols * rows, block).astype(jnp.bfloat16)]
    select_n x17 -> x0, other arithmetic: 13.8 us -> none  [the longest x1 8.01 us: body(): pos = jnp.where(inside, jnp.take(pos_piece, local, axis=1), blank)]
    unnamed x10, local copies, waits for them, and re-layouts: 7.82 us -> 1.34 us
    convert_element_type x8 -> x0, other arithmetic: 4.96 us -> none  [one_block(): factor = factor.reshape(3 * cols * rows, block).astype(jnp.bfloat16)]
  transfers between devices with their start and end apart: 6 -> 5, of which waited for: 3 -> 1; matrix products, arithmetic and copies ran while one was open for 0% -> 0% of each run, Pallas kernels for 0% -> 18%
where the time goes in v1:
time: 31.5 us; the launch traced here: 31.3 us
  Pallas kernels  18.1 us (57%)
  starting transfers between devices  8.21 us (26%)
  waiting for transfers between devices  3.56 us (11%)
  local copies, waits for them, and re-layouts  1.34 us (4%)
    pallas_call x1, Pallas kernels, body(): pl.pallas_call(functools.partial(with_accumulators, functools.partial(fin...  10.2 us
    pallas_call x1, Pallas kernels, body(): pl.pallas_call(functools.partial(with_accumulators, own_kernel, naccs, de...  5.71 us
    ppermute x3, starting transfers between devices, body(): received[m] = lax.ppermute(value, 'brick', pairs)  5.64 us
    ppermute x3, waiting for transfers between devices, body(): received[m] = lax.ppermute(value, 'brick', pairs)  3.55 us
    ppermute x1, starting transfers between devices, body(): lax.ppermute(xb, 'region', [(r, (r + (1 if r % 2 else -1)) % regions) for...  2.56 us
    pallas_call x1, Pallas kernels, body(): pl.pallas_call(functools.partial(pack_kernel, bricks), out_shape=(markers...  2.19 us
    unnamed x10, local copies, waits for them, and re-layouts  1.34 us
  transfers between devices with their start and end apart: 5, of which 1 were waited for; matrix products, arithmetic and copies ran while one was open for 0% of the time, Pallas kernels for 18%

profile of v1, /device:TPU:0, one launch (start us, length us, event | category | flops | bytes accessed | tf_op | source)
XLA Modules:
  0.0 31.3 jit_solution(10322036934486411365)
XLA Ops:
  0.0 2.2 %pack.1 = (f32[192,128]{1,0:T(8,128)}, f32[320,128]{1,0:T(8,128)}, f32[320,128]{1,0:T(8,128)}, f32[4,16,256]{2,1,0:T(8,128)}, f32[4,16,256]{2,1,0:T(8,128)}) custom-call(f32[3,16,16,256]{3,2,1,0:T(8,128)} %refs_0_.1, f32[16,16,256]{2,1,0:T(8,128)} %refs_1_.1, f32[3,4096]{1,0:T(4,128)} %pos_ref.1, f32[3,4096]{1,0:T(4,128)} %force_ref.1), custom_call_target="tpu_custom_call" | custom-call | tf_op jit(solution)/shard_map/pack/pallas_call | solution.py:331
  2.2 3.1 %collective-permute-start.2 = (f32[320,128]{1,0:T(8,128)}, f32[320,128]{1,0:T(8,128)S(1)}, u32[]{:S(2)}, u32[]{:S(2)}) collective-permute-start(f32[320,128]{1,0:T(8,128)} %get-tuple-element.11.refs_1_), channel_id=1, source_target_pairs={{0,1},{1,0},{2,3},{3,2},{4,5},{5,4},{6,7},{7,6},{8,9},{9,8},{10,11... | collective-permute-start | bytes 491528 | tf_op jit(solution)/shard_map/ppermute | solution.py:348
  5.2 2.5 %collective-permute-start.4 = (f32[320,128]{1,0:T(8,128)}, f32[320,128]{1,0:T(8,128)S(1)}, u32[]{:S(2)}, u32[]{:S(2)}) collective-permute-start(f32[320,128]{1,0:T(8,128)} %get-tuple-element.12.refs_2_), channel_id=1, source_target_pairs={{0,3},{1,2},{2,1},{3,0},{4,7},{5,6},{6,5},{7,4},{8,11},{9,10},{10,... | collective-permute-start | bytes 491528 | tf_op jit(solution)/shard_map/ppermute | solution.py:348
  7.7 0.1 collective-permute-start.3
  7.8 0.0 collective-permute-start
  7.8 2.6 %collective-permute-start.1 = (f32[4,16,256]{2,1,0:T(8,128)}, f32[4,16,256]{2,1,0:T(8,128)S(1)}, u32[]{:S(2)}, u32[]{:S(2)}) collective-permute-start(f32[4,16,256]{2,1,0:T(8,128)} %get-tuple-element.14.refs_4_), channel_id=1, source_target_pairs={{0,28},{4,8},{8,4},{12,16},{16,12},{20,24},{24,20},{28,0},{1,29},{... | collective-permute-start | bytes 196616 | tf_op jit(solution)/shard_map/ppermute | solution.py:350
  10.4 5.7 %own.1.refs_0_ = f32[3,16,16,256]{3,2,1,0:T(8,128)} custom-call(f32[3,16,16,256]{3,2,1,0:T(8,128)} %refs_0_.1, f32[16,16,256]{2,1,0:T(8,128)} %refs_1_.1, f32[192,128]{1,0:T(8,128)} %get-tuple-element.10.refs_2_), custom_call_target="tpu_custom_call" | custom-call | tf_op jit(solution)/shard_map/own/pallas_call | solution.py:357
  16.1 0.0 collective-permute-done.refs_5_
  16.1 0.0 copy-start.3
  16.1 0.0 collective-permute-done.1.refs_6_
  16.1 0.0 copy-start.4
  16.1 3.5 %collective-permute-done.3.refs_8_ = f32[192,128]{1,0:T(8,128)S(1)} collective-permute-done((f32[192,128]{1,0:T(8,128)}, f32[192,128]{1,0:T(8,128)S(1)}, u32[]{:S(2)}, u32[]{:S(2)}) %collective-permute-start.3) | collective-permute-done | bytes 98336 | tf_op jit(solution)/shard_map/ppermute | solution.py:348
  19.7 0.0 copy-start.2
  19.7 0.0 collective-permute-done.2.refs_7_
  19.7 0.0 copy-start
  19.7 0.0 collective-permute-done.4.refs_9_
  19.7 0.0 copy-done.3
  19.7 0.0 copy-done.4
  19.7 0.6 %copy-done.2 = f32[192,128]{1,0:T(8,128)} copy-done((f32[192,128]{1,0:T(8,128)}, f32[192,128]{1,0:T(8,128)S(1)}, u32[]{:S(2)}) %copy-start.2) | copy-done | bytes 98328
  20.3 0.1 copy-done
  20.4 0.0 copy-start.1
  20.4 0.7 %copy-done.1 = f32[320,128]{1,0:T(8,128)} copy-done((f32[320,128]{1,0:T(8,128)}, f32[320,128]{1,0:T(8,128)S(1)}, u32[]{:S(2)}) %copy-start.1) | copy-done | bytes 163864
  21.0 10.2 %final.1 = f32[3,16,16,256]{3,2,1,0:T(8,128)} custom-call(f32[3,16,16,256]{3,2,1,0:T(8,128)} %own.1.refs_0_, f32[320,128]{1,0:T(8,128)} %get-tuple-element.11.refs_1_, f32[320,128]{1,0:T(8,128)} %get-tuple-element.12.refs_2_, f32[4,16,256]{2,1,0:T(8,128)} %get-tuple-element.13.refs_3_, f32[4,16,256]{2,1,0:T(8,128)} %get-tuple-element.14.refs_4_, ...), custom_call_target="tpu_custom_call" | custom-call | tf_op jit(solution)/shard_map/final/pallas_call | solution.py:367
Async XLA Ops:
  2.2 17.5 %collective-permute-start.2 = (f32[320,128]{1,0:T(8,128)}, f32[320,128]{1,0:T(8,128)S(1)}, u32[]{:S(2)}, u32[]{:S(2)}) collective-permute-start(f32[320,128]{1,0:T(8,128)} %get-tuple-element.11.refs_1_), channel_id=1, source_target_pairs={{0,1},{1,0},{2,3},{3,2},{4,5},{5,4},{6,7},{7,6},{8,9},{9,8},{10,11... | collective-permute-start | bytes 491528 | tf_op jit(solution)/shard_map/ppermute | solution.py:348
  5.2 14.5 %collective-permute-start.4 = (f32[320,128]{1,0:T(8,128)}, f32[320,128]{1,0:T(8,128)S(1)}, u32[]{:S(2)}, u32[]{:S(2)}) collective-permute-start(f32[320,128]{1,0:T(8,128)} %get-tuple-element.12.refs_2_), channel_id=1, source_target_pairs={{0,3},{1,2},{2,1},{3,0},{4,7},{5,6},{6,5},{7,4},{8,11},{9,10},{10,... | collective-permute-start | bytes 491528 | tf_op jit(solution)/shard_map/ppermute | solution.py:348
  7.7 12.0 %collective-permute-start.3 = (f32[192,128]{1,0:T(8,128)}, f32[192,128]{1,0:T(8,128)S(1)}, u32[]{:S(2)}, u32[]{:S(2)}) collective-permute-start(f32[192,128]{1,0:T(8,128)} %get-tuple-element.10.refs_2_), channel_id=1, source_target_pairs={{0,2},{1,3},{2,0},{3,1},{4,6},{5,7},{6,4},{7,5},{8,10},{9,11},{10,... | collective-permute-start | bytes 294920 | tf_op jit(solution)/shard_map/ppermute | solution.py:348
  7.8 8.3 %collective-permute-start = (f32[4,16,256]{2,1,0:T(8,128)}, f32[4,16,256]{2,1,0:T(8,128)S(1)}, u32[]{:S(2)}, u32[]{:S(2)}) collective-permute-start(f32[4,16,256]{2,1,0:T(8,128)} %get-tuple-element.13.refs_3_), channel_id=1, source_target_pairs={{0,4},{4,0},{8,12},{12,8},{16,20},{20,16},{24,28},{28,24},{1,5},{5... | collective-permute-start | bytes 196616 | tf_op jit(solution)/shard_map/ppermute | solution.py:349
  7.8 8.3 %collective-permute-start.1 = (f32[4,16,256]{2,1,0:T(8,128)}, f32[4,16,256]{2,1,0:T(8,128)S(1)}, u32[]{:S(2)}, u32[]{:S(2)}) collective-permute-start(f32[4,16,256]{2,1,0:T(8,128)} %get-tuple-element.14.refs_4_), channel_id=1, source_target_pairs={{0,28},{4,8},{8,4},{12,16},{16,12},{20,24},{24,20},{28,0},{1,29},{... | collective-permute-start | bytes 196616 | tf_op jit(solution)/shard_map/ppermute | solution.py:350
  16.1 3.6 %copy-start.3 = (f32[4,16,256]{2,1,0:T(8,128)}, f32[4,16,256]{2,1,0:T(8,128)S(1)}, u32[]{:S(2)}) copy-start(f32[4,16,256]{2,1,0:T(8,128)S(1)} %collective-permute-done.refs_5_) | copy-start | bytes 196612
  16.1 3.6 %copy-start.4 = (f32[4,16,256]{2,1,0:T(8,128)}, f32[4,16,256]{2,1,0:T(8,128)S(1)}, u32[]{:S(2)}) copy-start(f32[4,16,256]{2,1,0:T(8,128)S(1)} %collective-permute-done.1.refs_6_) | copy-start | bytes 196612
  19.7 0.6 %copy-start.2 = (f32[192,128]{1,0:T(8,128)}, f32[192,128]{1,0:T(8,128)S(1)}, u32[]{:S(2)}) copy-start(f32[192,128]{1,0:T(8,128)S(1)} %collective-permute-done.3.refs_8_) | copy-start | bytes 294916
  19.7 0.7 %copy-start = (f32[320,128]{1,0:T(8,128)}, f32[320,128]{1,0:T(8,128)S(1)}, u32[]{:S(2)}) copy-start(f32[320,128]{1,0:T(8,128)S(1)} %collective-permute-done.2.refs_7_) | copy-start | bytes 491524
  20.4 0.7 %copy-start.1 = (f32[320,128]{1,0:T(8,128)}, f32[320,128]{1,0:T(8,128)S(1)}, u32[]{:S(2)}) copy-start(f32[320,128]{1,0:T(8,128)S(1)} %collective-permute-done.4.refs_9_) | copy-start | bytes 491524

commit v2 on v1

v2 whole, which is shorter than its diff:
```python
import functools
import math

import jax
import jax.numpy as jnp
from jax import lax
from jax.experimental import pallas as pl
from jax.experimental.pallas import tpu as pltpu
from jax.sharding import PartitionSpec as P

LANES = 128
NQ = 24
GRANT = 16 << 20


def poly(t, coefs):
    out = jnp.full_like(t, coefs[-1])
    for c in coefs[-2::-1]:
        out = out * t + c
    return out


COS_COEFS = [(-1.0) ** n / math.factorial(2 * n) for n in range(8)]
SIN_COEFS = [(-1.0) ** n / math.factorial(2 * n + 1) for n in range(8)]


def window(u):
    shifted = u - 0.5
    cell = jnp.floor(shifted)
    angle = (0.5 * math.pi) * (shifted - cell)
    sq = angle * angle
    cosine = poly(sq, COS_COEFS)
    sine = angle * poly(sq, SIN_COEFS)
    first = cell - 1.0
    weights = (0.25 - 0.25 * sine, 0.25 + 0.25 * cosine, 0.25 + 0.25 * sine, 0.25 - 0.25 * cosine)
    residue = first - 4.0 * jnp.floor(first * 0.25)
    is_res = [residue == float(m) for m in range(4)]
    by_res = []
    for m in range(4):
        w = weights[3]
        for a in (2, 1, 0):
            w = jnp.where(is_res[(m - a) % 4], weights[a], w)
        by_res.append(w)
    return first, by_res


def prepare(mk_ref, prep_ref, at, groups, total, x_low, y_low):
    def part(q):
        return mk_ref[q * groups:(q + 1) * groups, :]

    def put(q, value):
        prep_ref[q * total + at:q * total + at + groups, :] = value

    z_first, z_w = window(part(2))
    block = jnp.floor(z_first * (1.0 / 16.0))
    put(0, block)
    put(1, z_first - 16.0 * block)
    for m in range(4):
        put(2 + m, z_w[m])
    y_first, y_w = window(part(1) - y_low)
    put(6, y_first)
    for m in range(4):
        put(7 + m, y_w[m])
    x_first, x_w = window(part(0) - x_low)
    put(11, x_first)
    for c in range(3):
        force = part(3 + c)
        for m in range(4):
            put(12 + 4 * c + m, force * x_w[m])


def spread(prep_ref, total, accs, cols, rows, depth, beside=None):
    sub = lax.broadcasted_iota(jnp.int32, (8, LANES), 0)
    subf = sub.astype(jnp.float32)
    phase = sub & 3
    zero16 = jnp.zeros((16, LANES), jnp.bfloat16)

    def wide(q, g):
        return jnp.broadcast_to(prep_ref[pl.ds(q * total + g, 1), :], (8, LANES))

    def pattern(q, g):
        w = wide(q + 3, g)
        for m in (2, 1, 0):
            w = jnp.where(phase == m, wide(q + m, g), w)
        return w

    def packed(a, b):
        return jnp.concatenate([a, b], axis=0).astype(jnp.bfloat16)

    def push(tile, mxu):
        zcols = []
        for g in (2 * tile, 2 * tile + 1):
            w = pattern(2, g)
            zero = jnp.zeros_like(w)
            d0 = subf - wide(1, g)
            lo0 = jnp.where((d0 >= 0.0) & (d0 <= 3.0), w, zero)
            lo1 = jnp.where((d0 >= -8.0) & (d0 <= -5.0), w, zero)
            hi0 = jnp.where(d0 <= -13.0, w, zero)
            low = packed(lo0, lo1)
            high = packed(hi0, zero)
            blk = wide(0, g)
            blk16 = packed(blk, blk)
            prev = None
            col = []
            for t in range(depth // 16):
                here = blk16 == jnp.bfloat16(t)
                v = zero16 if prev is None else jnp.where(prev, high, zero16)
                col.append(jnp.where(here, low, v))
                prev = here
            zcols.append(jnp.concatenate(col, axis=0))
        pltpu.matmul_push_rhs(jnp.concatenate(zcols, axis=1), 0, mxu, transpose=True)

    def stream(pair, following):
        wys, xfirst = [], []
        for mxu in range(2):
            tile = 2 * pair + mxu
            wys.append([])
            xfirst.append([])
            for g in (2 * tile, 2 * tile + 1):
                w = pattern(7, g)
                zero = jnp.zeros_like(w)
                d0 = subf - wide(6, g)
                halves = []
                for h in range(rows // 8):
                    d = d0 + 8.0 * h
                    halves.append(jnp.where((d >= 0.0) & (d <= 3.0), w, zero))
                wys[mxu].append(halves)
                xf = wide(11, g)
                xfirst[mxu].append(packed(xf, xf))
        first = True
        for m in range(4):
            inside = [
                {
                    i: [(xf <= jnp.bfloat16(i)) & (xf >= jnp.bfloat16(i - 3)) for xf in xfirst[mxu]]
                    for i in range(m, cols, 4)
                }
                for mxu in range(2)
            ]
            for c in range(3):
                for rb in range(rows // 16):
                    for mxu in range(2):
                        tile = 2 * pair + mxu
                        quad = []
                        for n in range(2):
                            f = wide(12 + 4 * c + m, 2 * tile + n)
                            wy = wys[mxu][n]
                            quad.append(packed(f * wy[2 * rb], f * wy[2 * rb + 1]))
                        for i in range(m, cols, 4):
                            lhs = jnp.concatenate(
                                [jnp.where(inside[mxu][i][n], quad[n], zero16) for n in range(2)],
                                axis=1,
                            )
                            pltpu.matmul_acc_lhs(
                                accs[mxu][(c * cols + i) * (rows // 16) + rb], lhs,
                                load_staged_rhs=0 if first and i == m else None,
                            )
                    if first and following is not None:
                        for mxu in range(2):
                            push(2 * following + mxu, mxu)
                    first = False

    pairs = total // 4
    for mxu in range(2):
        push(mxu, mxu)

    def step(t, carry):
        stream(t, t + 1)
        if beside is not None:
            beside(t)
        return carry

    lax.fori_loop(0, pairs - 1, step, 0)
    stream(pairs - 1, None)
    if beside is not None:
        beside(pairs - 1)


def corner(cols, rows):
    region = lax.axis_index("region")
    brick = lax.axis_index("brick")
    return (region * cols).astype(jnp.float32), (brick * rows).astype(jnp.float32)


def pack_kernel(vel_hbm, visc_hbm, pos_hbm, force_hbm, mk_ref, s1_ref, s3_ref, xa_ref, xb_ref,
                vel_ref, visc_ref, pos_ref, force_ref, sems):
    copies = [
        pltpu.make_async_copy(src, dst, sems.at[n])
        for n, (src, dst) in enumerate((
            (pos_hbm, pos_ref), (force_hbm, force_ref), (vel_hbm, vel_ref), (visc_hbm, visc_ref)
        ))
    ]
    for copy in copies:
        copy.start()
    cols, rows, depth = visc_ref.shape
    groups = pos_ref.shape[1] // LANES
    brick_odd = (lax.axis_index("brick") & 1) == 1
    region_odd = (lax.axis_index("region") & 1) == 1
    for first, copy, src in ((0, copies[0], pos_ref), (3, copies[1], force_ref)):
        copy.wait()
        for c in range(3):
            for g in range(groups):
                row = src[c:c + 1, g * LANES:(g + 1) * LANES]
                at = (first + c) * groups + g
                mk_ref[at:at + 1, :] = row
                s1_ref[at:at + 1, :] = row
                s3_ref[at:at + 1, :] = row
    copies[2].wait()
    copies[3].wait()

    def plane(c, i):
        return vel_ref[c, i] if c < 3 else visc_ref[i]

    base = 6 * groups
    for c in range(4):
        low, high = plane(c, 0), plane(c, cols - 1)
        xa_ref[c] = jnp.where(region_odd, low, high)
        xb_ref[c] = jnp.where(region_odd, high, low)
        for i in range(cols):
            low = vel_ref[c, i, 0:1, :] if c < 3 else visc_ref[i, 0:1, :]
            high = vel_ref[c, i, rows - 1:rows, :] if c < 3 else visc_ref[i, rows - 1:rows, :]
            one = jnp.where(brick_odd, low, high)
            other = jnp.where(brick_odd, high, low)
            for h in range(depth // LANES):
                at = base + (h * 4 + c) * cols + i
                lane = slice(h * LANES, (h + 1) * LANES)
                s1_ref[at:at + 1, :] = one[:, lane]
                s3_ref[at:at + 1, :] = other[:, lane]


def pop(accs, index):
    return pltpu.matmul_pop(accs[0][index]) + pltpu.matmul_pop(accs[1][index])


def with_accumulators(kernel, naccs, depth, *refs):
    def run(*accs):
        kernel((accs[:naccs], accs[naccs:]), *refs)

    pl.run_scoped(
        run,
        *(pltpu.ACC(mxu)((16, depth), jnp.float32) for mxu in range(2) for _ in range(naccs)),
    )


def own_kernel(accs, vel_ref, visc_ref, mk_ref, base_ref, prep_ref):
    cols, rows, depth = visc_ref.shape
    groups = mk_ref.shape[0] // 6
    x_low, y_low = corner(cols, rows)
    prepare(mk_ref, prep_ref, 0, groups, groups, x_low, y_low)
    lane = lax.broadcasted_iota(jnp.int32, (rows, depth), 1)
    at_low, at_high = lane == 0, lane == depth - 1
    zero = jnp.zeros((rows, depth), jnp.float32)

    def rolled(p):
        return (
            pltpu.roll(p, rows - 1, 0), pltpu.roll(p, 1, 0),
            pltpu.roll(p, depth - 1, 1), pltpu.roll(p, 1, 1),
        )

    def plane(i):
        up = jnp.minimum(i + 1, cols - 1)
        down = jnp.maximum(i - 1, 0)
        mu = 0.05 * visc_ref[i]
        v = [vel_ref[d, i] for d in range(3)]
        mu_n = (0.05 * visc_ref[up], 0.05 * visc_ref[down]) + rolled(mu)
        pairs = [mu + p for p in mu_n]
        pairs[4] = jnp.where(at_high, mu, pairs[4])
        pairs[5] = jnp.where(at_low, mu, pairs[5])
        centre = 1.0 - (((pairs[0] + pairs[1]) + (pairs[2] + pairs[3])) + (pairs[4] + pairs[5]))
        gain = []
        for d in range(3):
            along = 0.05 * v[d]
            gain += [pairs[2 * d] - along, pairs[2 * d + 1] + along]
        gain[4] = jnp.where(at_high, zero, gain[4])
        gain[5] = jnp.where(at_low, zero, gain[5])
        for c in range(3):
            near = (vel_ref[c, up], vel_ref[c, down]) + rolled(v[c])
            value = centre * v[c]
            for g, u in zip(gain, near):
                value = value + g * u
            base_ref[c, i] = value

    pairs = groups // 4
    each = -(-cols // pairs)

    def beside(t):
        for n in range(each):
            plane(jnp.minimum(each * t + n, cols - 1))

    spread(prep_ref, groups, accs, cols, rows, depth, beside)
    for c in range(3):
        for i in range(cols):
            base_ref[c, i] += 0.1 * pop(accs, c * cols + i)


def add_shards(shards, prep_ref, accs, groups, cols, rows, depth):
    x_low, y_low = corner(cols, rows)
    total = len(shards) * groups
    for n, mk_ref in enumerate(shards):
        prepare(mk_ref, prep_ref, n * groups, groups, total, x_low, y_low)
    spread(prep_ref, total, accs, cols, rows, depth)


def more_kernel(groups, accs, base_ref, *refs):
    *shards, out_ref, prep_ref = refs
    _, cols, rows, depth = base_ref.shape
    add_shards(shards, prep_ref, accs, groups, cols, rows, depth)
    for c in range(3):
        for i in range(cols):
            out_ref[c, i] = base_ref[c, i] + 0.1 * pop(accs, c * cols + i)


def final_kernel(groups, face_of, accs, base_ref, s1_ref, s3_ref, xa_ref, xb_ref, ra_ref, rb_ref, *refs):
    nfaces = len(face_of)
    faces, refs = refs[:nfaces], refs[nfaces:]
    *shards, out_hbm, out_ref, prep_ref, sems = refs
    _, cols, rows, depth = base_ref.shape
    add_shards(shards, prep_ref, accs, groups, cols, rows, depth)

    region = lax.axis_index("region")
    regions = lax.axis_size("region")
    brick = lax.axis_index("brick")
    region_odd = (region & 1) == 1
    brick_odd = (brick & 1) == 1
    has_low = region > 0
    has_high = region < regions - 1

    def fix(sign, own, d, c, far, taken):
        mu, u = own[3], own[c]
        along = mu - own[d] if sign > 0 else mu + own[d]
        return 0.05 * (
            along * (far[c] - taken[c]) + far[3] * (far[c] - u) - taken[3] * (taken[c] - u)
        )

    zero = jnp.zeros((rows, depth), jnp.float32)
    own_high = [jnp.where(region_odd, xb_ref[c], xa_ref[c]) for c in range(4)]
    own_low = [jnp.where(region_odd, xa_ref[c], xb_ref[c]) for c in range(4)]
    far_high = [jnp.where(has_high, jnp.where(region_odd, rb_ref[c], ra_ref[c]), zero) for c in range(4)]
    far_low = [jnp.where(has_low, jnp.where(region_odd, ra_ref[c], rb_ref[c]), zero) for c in range(4)]

    base = 6 * groups

    def face(ref, h, c):
        return ref[base + (h * 4 + c) * cols:base + (h * 4 + c + 1) * cols, :]

    none = jnp.zeros((cols, LANES), jnp.float32)
    top, low = {}, {}
    for h in range(depth // LANES):
        own_one = [face(s1_ref, h, c) for c in range(4)]
        own_two = [face(s3_ref, h, c) for c in range(4)]
        far_one, far_two = [none] * 4, [none] * 4
        for ref, m in zip(faces, face_of):
            got = [face(ref, h, c) for c in range(4)]
            if m == 1:
                far_one = got
            else:
                partner = brick ^ m
                good = (partner - brick == 1) | (brick - partner == 1)
                far_two = [jnp.where(good, g, f) for g, f in zip(got, far_two)]
        high_own = [jnp.where(brick_odd, b, a) for a, b in zip(own_one, own_two)]
        low_own = [jnp.where(brick_odd, a, b) for a, b in zip(own_one, own_two)]
        high_far = [jnp.where(brick_odd, b, a) for a, b in zip(far_one, far_two)]
        low_far = [jnp.where(brick_odd, a, b) for a, b in zip(far_one, far_two)]
        for c in range(3):
            top[c, h] = fix(1, high_own, 1, c, high_far, low_own)
            low[c, h] = fix(-1, low_own, 1, c, low_far, high_own)

    for c in range(3):
        for i in range(cols):
            value = base_ref[c, i] + 0.1 * pop(accs, c * cols + i)
            if i == 0:
                value = value + fix(-1, own_low, 0, c, far_low, own_low)
            if i == cols - 1:
                value = value + fix(1, own_high, 0, c, far_high, own_high)
            out_ref[c, i] = value
            for h in range(depth // LANES):
                lane = slice(h * LANES, (h + 1) * LANES)
                out_ref[c, i, rows - 1:rows, lane] += top[c, h][i:i + 1]
                out_ref[c, i, 0:1, lane] += low[c, h][i:i + 1]
        pltpu.make_async_copy(out_ref.at[c], out_hbm.at[c], sems.at[c]).start()
    for c in range(3):
        pltpu.make_async_copy(out_ref.at[c], out_hbm.at[c], sems.at[c]).wait()


def body(velocity, viscosity, marker_pos, marker_force, slot_lists):
    del slot_lists
    cols, rows, depth = viscosity.shape
    bricks = lax.axis_size("brick")
    regions = lax.axis_size("region")
    groups = marker_pos.shape[1] // LANES
    f32 = jnp.float32
    vmem = pl.BlockSpec(memory_space=pltpu.VMEM)
    hbm = pl.BlockSpec(memory_space=pltpu.HBM)
    params = pltpu.CompilerParams(vmem_limit_bytes=GRANT)
    markers = jax.ShapeDtypeStruct((6 * groups, LANES), f32)
    with_face = jax.ShapeDtypeStruct((6 * groups + 8 * cols, LANES), f32)
    xface = jax.ShapeDtypeStruct((4, rows, depth), f32)
    field = jax.ShapeDtypeStruct(velocity.shape, f32)
    mk, s1, s3, xa, xb = pl.pallas_call(
        pack_kernel,
        out_shape=(markers, with_face, with_face, xface, xface),
        in_specs=[hbm] * 4,
        out_specs=(vmem,) * 5,
        scratch_shapes=[
            pltpu.VMEM(x.shape, f32) for x in (velocity, viscosity, marker_pos, marker_force)
        ] + [pltpu.SemaphoreType.DMA((4,))],
        compiler_params=params,
        name="pack",
    )(*(
        pltpu.with_memory_space_constraint(x, pltpu.HBM)
        for x in (velocity, viscosity, marker_pos, marker_force)
    ))

    partners = list(range(1, bricks))
    face_of = [m for m in partners if m & (m + 1) == 0]
    received = {}
    for m in sorted(partners, key=lambda m: m in face_of):
        value = mk if m not in face_of else s1 if m == 1 else s3
        received[m] = lax.ppermute(value, "brick", [(b, b ^ m) for b in range(bricks)])
    ra = lax.ppermute(xa, "region", [(r, r ^ 1) for r in range(regions)])
    rb = lax.ppermute(
        xb, "region", [(r, (r + (1 if r % 2 else -1)) % regions) for r in range(regions)]
    )

    naccs = 3 * cols * rows // 16

    def prep(shards):
        return pltpu.VMEM((NQ * groups * shards, LANES), f32)

    base = pl.pallas_call(
        functools.partial(with_accumulators, own_kernel, naccs, depth),
        out_shape=field,
        in_specs=[vmem] * 3,
        out_specs=vmem,
        scratch_shapes=[prep(1)],
        compiler_params=params,
        name="own",
    )(velocity, viscosity, mk)

    early, late = partners[:1], partners[1:]
    if late:
        base = pl.pallas_call(
            functools.partial(
                with_accumulators, functools.partial(more_kernel, groups), naccs, depth
            ),
            out_shape=field,
            in_specs=[vmem] * (1 + len(early)),
            out_specs=vmem,
            scratch_shapes=[prep(len(early))],
            compiler_params=params,
            name="more",
        )(base, *(received[m] for m in early))
    else:
        late = early
    return pl.pallas_call(
        functools.partial(
            with_accumulators, functools.partial(final_kernel, groups, face_of), naccs, depth
        ),
        out_shape=field,
        in_specs=[vmem] * (7 + len(face_of) + len(late)),
        out_specs=hbm,
        scratch_shapes=[
            pltpu.VMEM(velocity.shape, f32), prep(len(late)), pltpu.SemaphoreType.DMA((3,))
        ],
        compiler_params=params,
        name="final",
    )(base, s1, s3, xa, xb, ra, rb, *(received[m] for m in face_of), *(received[m] for m in late))


def solution(mesh):
    placed = (
        P(None, "region", "brick", None),
        P("region", "brick", None),
        P(None, ("region", "brick")),
        P(None, ("region", "brick")),
        P(("region", "brick"), None),
    )
    return jax.shard_map(
        body,
        mesh=mesh,
        in_specs=placed,
        out_specs=P(None, "region", "brick", None),
        check_vma=False,
    )
```

time: 31.5 us -> 23.9 us (0.76)
  Pallas kernels: 18.1 us -> 11.4 us
  local copies, waits for them, and re-layouts: 1.34 us -> 0.01 us
  waiting for transfers between devices: 3.56 us -> 4 us
    pallas_call x1, Pallas kernels: 10.2 us -> 4.93 us  [body(): pl.pallas_call(functools.partial(with_accumulators, functools.partial(fin...]
    pallas_call x1, Pallas kernels: 5.71 us -> 2.88 us  [body(): pl.pallas_call(functools.partial(with_accumulators, own_kernel, naccs, de...]
    pallas_call x1 -> x2, Pallas kernels: 2.19 us -> 3.64 us  [the longest x1 2.16 us: body(): pl.pallas_call(functools.partial(with_accumulators, functools.partial(mor...]
    unnamed x10 -> x4, local copies, waits for them, and re-layouts: 1.34 us -> 0.01 us
    ppermute x3, waiting for transfers between devices: 3.55 us -> 3.99 us  [body(): lax.ppermute(value, 'brick', [(b, b ^ m) for b in range(bricks)])]
  transfers between devices with their start and end apart: 5 -> 5, of which waited for: 1 -> 1; matrix products, arithmetic and copies ran while one was open for 0% -> 0% of each run, Pallas kernels for 18% -> 21%
where the time goes in v2:
time: 23.9 us; the launch traced here: 23.8 us
  Pallas kernels  11.4 us (48%)
  starting transfers between devices  8.27 us (35%)
  waiting for transfers between devices  4 us (17%)
    ppermute x3, starting transfers between devices, body(): lax.ppermute(value, 'brick', [(b, b ^ m) for b in range(bricks)])  5.71 us
    pallas_call x1, Pallas kernels, body(): pl.pallas_call(functools.partial(with_accumulators, functools.partial(fin...  4.93 us
    ppermute x3, waiting for transfers between devices, body(): lax.ppermute(value, 'brick', [(b, b ^ m) for b in range(bricks)])  3.99 us
    pallas_call x1, Pallas kernels, body(): pl.pallas_call(functools.partial(with_accumulators, own_kernel, naccs, de...  2.88 us
    ppermute x1, starting transfers between devices, body(): lax.ppermute(xb, 'region', [(r, (r + (1 if r % 2 else -1)) % regions) for...  2.56 us
    pallas_call x1, Pallas kernels, body(): pl.pallas_call(functools.partial(with_accumulators, functools.partial(mor...  2.16 us
    pallas_call x1, Pallas kernels, body(): pl.pallas_call(pack_kernel, out_shape=(markers, with_face, with_face, xfa...  1.49 us
  transfers between devices with their start and end apart: 5, of which 1 were waited for; matrix products, arithmetic and copies ran while one was open for 0% of the time, Pallas kernels for 21%

profile of v2, /device:TPU:0, one launch (start us, length us, event | category | flops | bytes accessed | tf_op | source)
XLA Modules:
  0.0 23.8 jit_solution(13791510708110583953)
XLA Ops:
  0.0 0.0 copy-start.1
  0.0 0.0 copy-start
  0.0 1.5 %pack.1 = (f32[192,128]{1,0:T(8,128)S(1)}, f32[320,128]{1,0:T(8,128)S(1)}, f32[320,128]{1,0:T(8,128)S(1)}, f32[4,16,256]{2,1,0:T(8,128)S(1)}, f32[4,16,256]{2,1,0:T(8,128)S(1)}) custom-call(f32[3,16,16,256]{3,2,1,0:T(8,128)} %refs_0_.1, f32[16,16,256]{2,1,0:T(8,128)} %refs_1_.1, f32[3,4096]{1,0:T(4,128)} %pos_hbm.1, f32[3,4096]{1,0:T(4,128)} %force_hbm.1), custom_call_target="tpu_custom_call" | custom-call | tf_op jit(solution)/shard_map/pack/pallas_call | solution.py:398
  1.5 3.1 %collective-permute-start = (f32[320,128]{1,0:T(8,128)S(1)}, f32[320,128]{1,0:T(8,128)S(1)}, u32[]{:S(2)}, u32[]{:S(2)}) collective-permute-start(f32[320,128]{1,0:T(8,128)S(1)} %get-tuple-element.11.refs_1_), channel_id=1, source_target_pairs={{0,1},{1,0},{2,3},{3,2},{4,5},{5,4},{6,7},{7,6},{8,9},{9,8},{10,11... | collective-permute-start | bytes 491528 | tf_op jit(solution)/shard_map/ppermute | solution.py:418
  4.6 2.5 %collective-permute-start.3 = (f32[320,128]{1,0:T(8,128)S(1)}, f32[320,128]{1,0:T(8,128)S(1)}, u32[]{:S(2)}, u32[]{:S(2)}) collective-permute-start(f32[320,128]{1,0:T(8,128)S(1)} %get-tuple-element.12.refs_2_), channel_id=1, source_target_pairs={{0,3},{1,2},{2,1},{3,0},{4,7},{5,6},{6,5},{7,4},{8,11},{9,10},{10,... | collective-permute-start | bytes 491528 | tf_op jit(solution)/shard_map/ppermute | solution.py:418
  7.1 0.1 collective-permute-start.4
  7.2 0.0 collective-permute-start.1
  7.2 2.6 %collective-permute-start.2 = (f32[4,16,256]{2,1,0:T(8,128)S(1)}, f32[4,16,256]{2,1,0:T(8,128)S(1)}, u32[]{:S(2)}, u32[]{:S(2)}) collective-permute-start(f32[4,16,256]{2,1,0:T(8,128)S(1)} %get-tuple-element.14.refs_4_), channel_id=1, source_target_pairs={{0,28},{4,8},{8,4},{12,16},{16,12},{20,24},{24,20},{28,0},{1,29},{... | collective-permute-start | bytes 196616 | tf_op jit(solution)/shard_map/ppermute | solution.py:420
  9.8 0.0 copy-done.1
  9.8 0.0 copy-done
  9.8 2.9 %own.1.refs_0_ = f32[3,16,16,256]{3,2,1,0:T(8,128)S(1)} custom-call(f32[3,16,16,256]{3,2,1,0:T(8,128)S(1)} %copy-done, f32[16,16,256]{2,1,0:T(8,128)S(1)} %copy-done.1, f32[192,128]{1,0:T(8,128)S(1)} %get-tuple-element.10.refs_2_), custom_call_target="tpu_custom_call" | custom-call | tf_op jit(solution)/shard_map/own/pallas_call | solution.py:429
  12.7 0.0 collective-permute-done.refs_1_.refs_7_
  12.7 2.2 %more.1.refs_0_ = f32[3,16,16,256]{3,2,1,0:T(8,128)S(1)} custom-call(f32[3,16,16,256]{3,2,1,0:T(8,128)S(1)} %own.1.refs_0_, f32[320,128]{1,0:T(8,128)S(1)} %collective-permute-done.refs_1_.refs_7_), custom_call_target="tpu_custom_call" | custom-call | tf_op jit(solution)/shard_map/more/pallas_call | solution.py:441
  14.8 0.0 collective-permute-done.1.refs_5_
  14.8 0.0 collective-permute-done.2.refs_6_
  14.9 4.0 %collective-permute-done.4.refs_9_ = f32[192,128]{1,0:T(8,128)S(1)} collective-permute-done((f32[192,128]{1,0:T(8,128)S(1)}, f32[192,128]{1,0:T(8,128)S(1)}, u32[]{:S(2)}, u32[]{:S(2)}) %collective-permute-start.4) | collective-permute-done | bytes 98336 | tf_op jit(solution)/shard_map/ppermute | solution.py:418
  18.8 0.0 collective-permute-done.3.refs_8_.refs_10_
  18.8 4.9 %final.1 = f32[3,16,16,256]{3,2,1,0:T(8,128)} custom-call(f32[3,16,16,256]{3,2,1,0:T(8,128)S(1)} %more.1.refs_0_, f32[320,128]{1,0:T(8,128)S(1)} %get-tuple-element.11.refs_1_, f32[320,128]{1,0:T(8,128)S(1)} %get-tuple-element.12.refs_2_, f32[4,16,256]{2,1,0:T(8,128)S(1)} %get-tuple-element.13.refs_3_, f32[4,16,256]{2,1,0:T(8,128)S(1)} %get-tuple-element.14.refs_4_, ...), custom_call_target="tpu_custom_call" | custom-call | tf_op jit(solution)/shard_map/final/pallas_call | solution.py:454
Async XLA Ops:
  0.0 9.8 %copy-start.1 = (f32[16,16,256]{2,1,0:T(8,128)S(1)}, f32[16,16,256]{2,1,0:T(8,128)}, u32[]{:S(2)}) copy-start(f32[16,16,256]{2,1,0:T(8,128)} %refs_1_.1) | copy-start | bytes 786436
  0.0 9.8 %copy-start = (f32[3,16,16,256]{3,2,1,0:T(8,128)S(1)}, f32[3,16,16,256]{3,2,1,0:T(8,128)}, u32[]{:S(2)}) copy-start(f32[3,16,16,256]{3,2,1,0:T(8,128)} %refs_0_.1) | copy-start | bytes 2359300
  1.5 11.2 %collective-permute-start = (f32[320,128]{1,0:T(8,128)S(1)}, f32[320,128]{1,0:T(8,128)S(1)}, u32[]{:S(2)}, u32[]{:S(2)}) collective-permute-start(f32[320,128]{1,0:T(8,128)S(1)} %get-tuple-element.11.refs_1_), channel_id=1, source_target_pairs={{0,1},{1,0},{2,3},{3,2},{4,5},{5,4},{6,7},{7,6},{8,9},{9,8},{10,11... | collective-permute-start | bytes 491528 | tf_op jit(solution)/shard_map/ppermute | solution.py:418
  4.6 14.2 %collective-permute-start.3 = (f32[320,128]{1,0:T(8,128)S(1)}, f32[320,128]{1,0:T(8,128)S(1)}, u32[]{:S(2)}, u32[]{:S(2)}) collective-permute-start(f32[320,128]{1,0:T(8,128)S(1)} %get-tuple-element.12.refs_2_), channel_id=1, source_target_pairs={{0,3},{1,2},{2,1},{3,0},{4,7},{5,6},{6,5},{7,4},{8,11},{9,10},{10,... | collective-permute-start | bytes 491528 | tf_op jit(solution)/shard_map/ppermute | solution.py:418
  7.1 11.8 %collective-permute-start.4 = (f32[192,128]{1,0:T(8,128)S(1)}, f32[192,128]{1,0:T(8,128)S(1)}, u32[]{:S(2)}, u32[]{:S(2)}) collective-permute-start(f32[192,128]{1,0:T(8,128)S(1)} %get-tuple-element.10.refs_2_), channel_id=1, source_target_pairs={{0,2},{1,3},{2,0},{3,1},{4,6},{5,7},{6,4},{7,5},{8,10},{9,11},{10,... | collective-permute-start | bytes 294920 | tf_op jit(solution)/shard_map/ppermute | solution.py:418
  7.2 7.6 %collective-permute-start.1 = (f32[4,16,256]{2,1,0:T(8,128)S(1)}, f32[4,16,256]{2,1,0:T(8,128)S(1)}, u32[]{:S(2)}, u32[]{:S(2)}) collective-permute-start(f32[4,16,256]{2,1,0:T(8,128)S(1)} %get-tuple-element.13.refs_3_), channel_id=1, source_target_pairs={{0,4},{4,0},{8,12},{12,8},{16,20},{20,16},{24,28},{28,24},{1,5},{5... | collective-permute-start | bytes 196616 | tf_op jit(solution)/shard_map/ppermute | solution.py:419
  7.2 7.6 %collective-permute-start.2 = (f32[4,16,256]{2,1,0:T(8,128)S(1)}, f32[4,16,256]{2,1,0:T(8,128)S(1)}, u32[]{:S(2)}, u32[]{:S(2)}) collective-permute-start(f32[4,16,256]{2,1,0:T(8,128)S(1)} %get-tuple-element.14.refs_4_), channel_id=1, source_target_pairs={{0,28},{4,8},{8,4},{12,16},{16,12},{20,24},{24,20},{28,0},{1,29},{... | collective-permute-start | bytes 196616 | tf_op jit(solution)/shard_map/ppermute | solution.py:420
